TPU v7x, 32 devices: a whole 2x2x4 slice. The times are simulated.
32 devices in a mesh: tgt: 4 (over y, x), sup: 8 (over z, core).
Axes of the slice: x: 2, y: 2, z: 4, core: 2. Of those that a mesh axis runs over, the one named last changes fastest.
Arguments:
- support: float32 [32, 3, 1024], P(('sup', 'tgt')), may hold values from -14 to 14
- coeffs: float32 [32, 100], P('sup'), may hold values from -10 to 10
- targets: float32 [32, 3, 1024], P(('tgt', 'sup')), may hold values from -14 to 14
- labels: float32 [32, 100], P(('tgt', 'sup')), may hold values from -5 to 5
Outputs:
- support_grad: float32 [32, 3, 1024], P(('sup', 'tgt'))
- residual: float32 [32, 100], P(('tgt', 'sup'))
All inputs are finite; a program needn't handle non-finite values.
Results may differ from a plain program's by a relative error of at most 0.000064.
Values sent between devices are 32-bit elements; how exact they have to be, the bound alone decides.
No kernel may reach another device: no remote copies, remote signals or barrier semaphores. Data moves between devices by JAX's collectives and lax.ppermute only.
A program may use at most 128 MiB of HBM per device.

v0:
```python
import math
import jax
import jax.numpy as jnp
from jax import lax
from jax.sharding import PartitionSpec as P

SIDE = 32
DEPTH = 3
WEIGHT_VAR = 1.6
BIAS_VAR = 0.1


def spread(values):
    side_cells = values.shape[0]
    padded = jnp.pad(values, ((1, 1), (1, 1), (0, 0)))
    summed = jnp.zeros_like(values)
    for row_shift in range(3):
        for col_shift in range(3):
            summed = (
                summed
                + padded[row_shift : row_shift + side_cells, col_shift : col_shift + side_cells]
            )
    return summed / 9.0


def self_levels(images):
    image_count = images.shape[0]
    energy = jnp.mean(images * images, axis=1)
    kernel_level = WEIGHT_VAR * spread(energy.T.reshape(SIDE, SIDE, image_count)) + BIAS_VAR
    levels = [kernel_level]
    for layer_idx in range(DEPTH - 1):
        activated = 2.0 / math.pi * jnp.arcsin(2.0 * kernel_level / (1.0 + 2.0 * kernel_level))
        kernel_level = WEIGHT_VAR * spread(activated) + BIAS_VAR
        levels.append(kernel_level)
    return levels


def pair_kernel(support, targets):
    sup_count = support.shape[0]
    tgt_count = targets.shape[0]
    sup_levels = self_levels(support)
    tgt_levels = self_levels(targets)
    products = (
        jnp.einsum("scp,tcp->pst", support, targets, precision=lax.Precision.HIGHEST)
        / support.shape[1]
    )
    kernel_level = (
        WEIGHT_VAR * spread(products.reshape(SIDE, SIDE, sup_count * tgt_count)) + BIAS_VAR
    )
    activated = kernel_level
    for layer_idx in range(DEPTH):
        sup_gain = lax.rsqrt(1.0 + 2.0 * sup_levels[layer_idx])
        tgt_gain = lax.rsqrt(1.0 + 2.0 * tgt_levels[layer_idx])
        correlation = (
            2.0
            * kernel_level.reshape(SIDE, SIDE, sup_count, tgt_count)
            * sup_gain[:, :, :, None]
            * tgt_gain[:, :, None, :]
        )
        activated = 2.0 / math.pi * jnp.arcsin(correlation)
        if layer_idx + 1 < DEPTH:
            kernel_level = (
                WEIGHT_VAR * spread(activated.reshape(SIDE, SIDE, sup_count * tgt_count)) + BIAS_VAR
            )
    return WEIGHT_VAR * jnp.mean(activated, axis=(0, 1)) + BIAS_VAR


def product(left, right):
    return jnp.dot(left, right, precision=lax.Precision.HIGHEST, preferred_element_type=jnp.float32)


def local(support, coeffs, targets, labels):
    tgt_dev = targets.shape[0]
    block = lax.all_gather(support, "tgt", axis=0, tiled=True)
    group, group_labels = (
        lax.all_gather(targets, "sup", axis=0, tiled=True),
        lax.all_gather(labels, "sup", axis=0, tiled=True),
    )
    theta, pullback = jax.vjp(lambda images: pair_kernel(images, group), block)
    predicted = lax.psum(product(theta.T, coeffs), "sup")
    misfit = predicted - group_labels
    residual = lax.dynamic_slice_in_dim(misfit, lax.axis_index("sup") * tgt_dev, tgt_dev, 0)
    block_grad = pullback(product(coeffs, misfit.T))[0]
    support_grad = lax.psum_scatter(block_grad, "tgt", scatter_dimension=0, tiled=True)
    return (support_grad, residual)


def solution(mesh):
    return jax.shard_map(
        local,
        mesh=mesh,
        in_specs=(
            P(("sup", "tgt"), None, None),
            P("sup", None),
            P(("tgt", "sup"), None, None),
            P(("tgt", "sup"), None),
        ),
        out_specs=(P(("sup", "tgt"), None, None), P(("tgt", "sup"), None)),
        check_vma=False,
    )
```

profile of v0, /device:TPU:0, one launch (start us, length us, event | category | flops | bytes accessed | tf_op | source)
XLA Modules:
  0.0 127.9 jit_solution(11291109133535098446)
XLA Ops:
  0.7 0.7 copy.146
  1.4 9.7 %all_gather.9 = f32[4,3,1024]{2,1,0:T(4,128)S(1)} all-gather(f32[1,3,1024]{2,1,0:T(4,128)S(1)} %copy.146), channel_id=1, replica_groups=mesh['tgt'=4,'sup'=8] {'tgt'}, dimensions={0}, use_global_device_ids=true | all-gather | bytes 61440 | tf_op jit(solution)/shard_map/all_gather | solution.py:74
  12.0 14.3 %all_gather.10 = f32[8,3,1024]{2,1,0:T(4,128)S(1)} all-gather(f32[1,3,1024]{2,1,0:T(4,128)S(1)} %copy.147), channel_id=1, replica_groups=mesh['tgt'=4,'sup'=8] {'sup'}, dimensions={0}, use_global_device_ids=true | all-gather | bytes 110592 | tf_op jit(solution)/shard_map/all_gather | solution.py:76
  26.8 0.9 add_rsqrt_fusion.1
  27.9 2.7 %copy.149 = f32[8,3,1024]{1,0,2:T(8,128)} copy(f32[8,3,1024]{2,1,0:T(4,128)S(1)} %all_gather.10) | data formatting | bytes 196608 | tf_op jit(solution)/shard_map/all_gather | solution.py:76
  30.6 1.8 %copy.148 = f32[4,3,1024]{1,0,2:T(4,128)} copy(f32[4,3,1024]{2,1,0:T(4,128)S(1)} %all_gather.9) | data formatting | bytes 98304 | tf_op jit(solution)/shard_map/all_gather | solution.py:74
  32.4 9.7 %convolution_multiply_fusion = f32[1024,4,8]{2,1,0:T(4,128)S(1)} fusion(f32[4,3,1024]{1,0,2:T(4,128)} %copy.148, f32[8,3,1024]{1,0,2:T(8,128)} %copy.149), kind=kOutput, calls=%fused_computation | convolution fusion | flops 1212416 | bytes 278528 | tf_op jit(solution)/shard_map/jvp(scp,tcp->pst)/dot_general | solution.py:44
  42.1 0.9 copy.150
  43.2 2.7 %add_multiply_fusion.3 = (f32[32,32,32]{1,0,2:T(8,128)S(1)}, f32[32,32,32]{1,0,2:T(8,128)S(1)}) fusion(f32[32,32,32]{1,2,0:T(8,128)S(1)} %get-tuple-element.40, f32[32,32,32]{1,2,0:T(8,128)S(1)} %get-tuple-element.41, f32[32,32,32]{1,0,2:T(8,128)S(1)} %reshape.78), kind=kLoop, calls=%fused_computation.116 | loop fusion | flops 589824 | bytes 655360 | tf_op jit(solution)/shard_map/jvp()/mul | solution.py:60
  45.9 0.7 add_multiply_fusion.11
  47.7 3.3 %add_multiply_fusion.1 = (f32[32,32,32]{1,0,2:T(8,128)S(1)}, f32[32,32,32]{1,0,2:T(8,128)}) fusion(f32[32,32,32]{1,2,0:T(8,128)S(1)} %get-tuple-element.42, f32[32,32,32]{1,2,0:T(8,128)S(1)} %get-tuple-element.43, f32[32,32,32]{1,0,2:T(8,128)S(1)} %get-tuple-element.26), kind=kLoop, calls=%fused_computation.114 | loop fusion | flops 589824 | bytes 655360 | tf_op jit(solution)/shard_map/jvp()/mul | solution.py:60
  51.0 0.7 add_multiply_fusion.9
  51.7 0.8 broadcast_multiply_fusion.2
  53.4 2.3 %multiply_reduce_fusion = (f32[32]{0:T(128)S(1)}, f32[32,32,32]{1,0,2:T(8,128)S(1)}) fusion(f32[32,32,32]{1,2,0:T(8,128)S(1)} %get-tuple-element.44, f32[32,32,32]{1,2,0:T(8,128)S(1)} %get-tuple-element.45, f32[32,32,32]{1,0,2:T(8,128)S(1)} %get-tuple-element.22), kind=kLoop, calls=%fused_computation.112 | loop fusion | flops 622560 | bytes 524416 | tf_op jit(solution)/shard_map/jvp()/reduce_sum | solution.py:65
  55.9 16.9 %psum.7 = f32[8,100]{1,0:T(8,128)S(1)} all-reduce(f32[8,100]{1,0:T(8,128)S(1)} %fusion.155), channel_id=1, replica_groups=mesh['tgt'=4,'sup'=8] {'sup'}, use_global_device_ids=true, to_apply=%region_3.4 | all-reduce | flops 800 | bytes 6400 | tf_op jit(solution)/shard_map/psum | solution.py:80
  72.8 8.6 %all-gather = f32[8,1,100]{2,1,0:T(1,128)S(1)} all-gather(f32[1,1,100]{2,1,0:T(1,128)S(1)} %bitcast.95), channel_id=1, replica_groups=mesh['tgt'=4,'sup'=8] {'sup'}, dimensions={0}, use_global_device_ids=true | all-gather | bytes 3600 | tf_op jit(solution)/shard_map/all_gather | solution.py:77
  81.6 1.4 %fusion.35 = f32[32,32,4]{1,2,0:T(4,128)S(1)} fusion(f32[32,32,32]{1,0,2:T(8,128)S(1)} %get-tuple-element.19, f32[4,8]{1,0:T(4,128)S(1)} %fusion, f32[32,32,8]{1,2,0:T(8,128)S(1)} %copy.169, f32[32,32,4]{1,2,0:T(4,128)} %copy-done.16), kind=kLoop, calls=%fused_computation.84 | loop fusion | flops 323584 | bytes 196736 | tf_op jit(solution)/shard_map/transpose(jvp())/reduce_sum | solution.py:55
  83.0 0.9 fusion.144
  83.9 0.9 broadcast_bitcast_fusion.2
  84.8 2.3 %fusion.47 = f32[32,32,32]{1,0,2:T(8,128)S(1)} fusion(f32[32,32,32]{1,2,0:T(8,128)} %broadcast_bitcast_fusion.2, f32[32,32,32]{1,2,0:T(8,128)S(1)} %get-tuple-element.44, f32[32]{0:T(128)S(1)} %broadcast_in_dim.16, f32[32,32,32]{1,0,2:T(8,128)S(1)} %get-tuple-element.19, f32[32,32,32]{1,2,0:T(8,128)S(1)} %get-tuple-element.45), kind=kLoop, calls=%fused_computation.105 | loop fusion | flops 294912 | bytes 655488 | tf_op jit(solution)/shard_map/transpose(jvp())/div | solution.py:23
  87.7 1.4 %fusion.46 = (f32[32,32,32]{1,0,2:T(8,128)S(1)}, f32[32,32,32]{1,0,2:T(8,128)S(1)}) fusion(f32[32,32,32]{1,2,0:T(8,128)S(1)} %broadcast_bitcast_fusion.1, f32[32,32,32]{1,2,0:T(8,128)S(1)} %copy-done.3, f32[32,32,32]{1,0,2:T(8,128)S(1)} %copy-done.1, f32[32,32,32]{1,2,0:T(8,128)S(1)} %copy-done.5, f32[32,32,32]{1,0,2:T(8,128)S(1)} %fusion.47, ...), kind=kLoop, calls=%fused_computation.103 | loop fusion | flops 524288 | bytes 1048576 | tf_op jit(solution)/shard_map/transpose(jvp())/div | solution.py:23
  89.7 1.5 %fusion.45 = (f32[32,32,32]{1,0,2:T(8,128)S(1)}, f32[32,32,32]{1,0,2:T(8,128)S(1)}) fusion(f32[32,32,32]{1,2,0:T(8,128)S(1)} %broadcast_bitcast_fusion, f32[32,32,32]{1,2,0:T(8,128)S(1)} %get-tuple-element.40, f32[32,32,32]{1,0,2:T(8,128)S(1)} %get-tuple-element.27, f32[32,32,32]{1,2,0:T(8,128)S(1)} %get-tuple-element.41, ...), kind=kLoop, calls=%fused_computation.101 | loop fusion | flops 524288 | bytes 1048576 | tf_op jit(solution)/shard_map/transpose(jvp())/div | solution.py:23
  91.2 0.8 fusion.43
  92.1 0.8 fusion.39
  94.3 0.8 fusion.31
  95.3 1.1 copy.180
  96.4 11.1 %fusion.156 = f32[1024,4,3]{1,2,0:T(4,128)} fusion(f32[1024,4,8]{2,1,0:T(4,128)S(1)} %copy.180, f32[8,3,1024]{1,0,2:T(8,128)} %copy.149), kind=kOutput, calls=%fused_computation.323 | convolution fusion | flops 1179648 | bytes 278528 | tf_op jit(solution)/shard_map/transpose(jvp(scp,tcp->pst))/dot_general | solution.py:44
  107.5 1.8 %copy.182 = f32[1024,4,3]{0,1,2:T(4,128)S(1)} copy(f32[1024,4,3]{1,2,0:T(4,128)} %fusion.156) | data formatting | bytes 98304 | tf_op jit(solution)/shard_map/transpose(jvp(scp,tcp->pst))/dot_general | solution.py:44
  109.5 16.1 %all-reduce.63 = f32[4,3,1024]{2,1,0:T(4,128)S(1)} all-reduce(f32[4,3,1024]{2,1,0:T(4,128)S(1)} %copy.192), channel_id=2, replica_groups=mesh['tgt'=4,'sup'=8] {'tgt'}, use_global_device_ids=true, to_apply=%region_7.8.clone | all-reduce | flops 12288 | bytes 98304
  125.5 0.6 dynamic-slice
  126.1 0.7 constant_dynamic-slice_fusion
  126.8 0.6 copy.193
  (96 shorter events, 7.3 us)
Async XLA Ops:
  0.6 55.1 %copy-start = (f32[4,100]{1,0:T(4,128)S(1)}, f32[4,100]{1,0:T(4,128)}, u32[]{:S(2)}) copy-start(f32[4,100]{1,0:T(4,128)} %param.5) | copy-start | bytes 4804
  0.6 11.3 %copy-start.20 = (f32[1,3,1024]{2,0,1:T(1,128)S(1)}, f32[1,3,1024]{2,0,1:T(1,128)}, u32[]{:S(2)}) copy-start(f32[1,3,1024]{2,0,1:T(1,128)} %param.6) | copy-start | bytes 36868
  11.1 19.5 %copy-start.6 = (f32[4,3,1024]{2,1,0:T(4,128)}, f32[4,3,1024]{2,1,0:T(4,128)S(1)}, u32[]{:S(2)}) copy-start(f32[4,3,1024]{2,1,0:T(4,128)S(1)} %all_gather.9) | copy-start | bytes 147460
  11.9 34.0 %copy-start.8 = (f32[32,32,4]{1,0,2:T(8,128)}, f32[32,32,4]{1,0,2:T(8,128)S(1)}, u32[]{:S(2)}) copy-start(f32[32,32,4]{1,0,2:T(8,128)S(1)} %get-tuple-element.29) | copy-start | bytes 49156
  12.0 15.9 %copy-start.12 = (f32[32,32,4]{1,2,0:T(4,128)}, f32[32,32,4]{1,2,0:T(4,128)S(1)}, u32[]{:S(2)}) copy-start(f32[32,32,4]{1,2,0:T(4,128)S(1)} %copy.155) | copy-start | bytes 49156
  43.0 3.9 %copy-start.17 = (f32[32,32,8]{1,0,2:T(8,128)S(1)}, f32[32,32,8]{1,0,2:T(8,128)}, u32[]{:S(2)}) copy-start(f32[32,32,8]{1,0,2:T(8,128)} %get-tuple-element.31) | copy-start | bytes 98308
  46.8 4.2 %copy-start.10 = (f32[32,32,4]{1,0,2:T(8,128)}, f32[32,32,4]{1,0,2:T(8,128)S(1)}, u32[]{:S(2)}) copy-start(f32[32,32,4]{1,0,2:T(8,128)S(1)} %get-tuple-element.25) | copy-start | bytes 49156
  46.9 4.1 %copy-start.14 = (f32[32,32,4]{1,2,0:T(4,128)}, f32[32,32,4]{1,2,0:T(4,128)S(1)}, u32[]{:S(2)}) copy-start(f32[32,32,4]{1,2,0:T(4,128)S(1)} %copy.163) | copy-start | bytes 49156
  47.7 5.7 %copy-start.2 = (f32[32,32,32]{1,2,0:T(8,128)}, f32[32,32,32]{1,2,0:T(8,128)S(1)}, u32[]{:S(2)}) copy-start(f32[32,32,32]{1,2,0:T(8,128)S(1)} %get-tuple-element.42) | copy-start | bytes 393220
  47.7 5.7 %copy-start.4 = (f32[32,32,32]{1,2,0:T(8,128)}, f32[32,32,32]{1,2,0:T(8,128)S(1)}, u32[]{:S(2)}) copy-start(f32[32,32,32]{1,2,0:T(8,128)S(1)} %get-tuple-element.43) | copy-start | bytes 393220
  52.6 3.1 %copy-start.16 = (f32[32,32,4]{1,2,0:T(4,128)}, f32[32,32,4]{1,2,0:T(4,128)S(1)}, u32[]{:S(2)}) copy-start(f32[32,32,4]{1,2,0:T(4,128)S(1)} %copy.167) | copy-start | bytes 49156
  52.6 20.2 %copy-start.21 = (f32[1,100]{1,0:T(1,128)S(1)}, f32[1,100]{1,0:T(1,128)}, u32[]{:S(2)}) copy-start(f32[1,100]{1,0:T(1,128)} %param.7) | copy-start | bytes 1204
  83.9 3.6 %copy-start.19 = (f32[32,32,4]{1,0,2:T(8,128)S(1)}, f32[32,32,4]{1,0,2:T(8,128)}, u32[]{:S(2)}) copy-start(f32[32,32,4]{1,0,2:T(8,128)} %get-tuple-element.37) | copy-start | bytes 49156
  84.8 2.8 %copy-start.1 = (f32[32,32,32]{1,0,2:T(8,128)S(1)}, f32[32,32,32]{1,0,2:T(8,128)}, u32[]{:S(2)}) copy-start(f32[32,32,32]{1,0,2:T(8,128)} %get-tuple-element.23) | copy-start | bytes 393220
  84.8 2.8 %copy-start.3 = (f32[32,32,32]{1,2,0:T(8,128)S(1)}, f32[32,32,32]{1,2,0:T(8,128)}, u32[]{:S(2)}) copy-start(f32[32,32,32]{1,2,0:T(8,128)} %copy-done.2) | copy-start | bytes 393220
  84.8 2.8 %copy-start.5 = (f32[32,32,32]{1,2,0:T(8,128)S(1)}, f32[32,32,32]{1,2,0:T(8,128)}, u32[]{:S(2)}) copy-start(f32[32,32,32]{1,2,0:T(8,128)} %copy-done.4) | copy-start | bytes 393220
  87.7 1.9 %copy-start.18 = (f32[32,32,4]{1,0,2:T(8,128)S(1)}, f32[32,32,4]{1,0,2:T(8,128)}, u32[]{:S(2)}) copy-start(f32[32,32,4]{1,0,2:T(8,128)} %get-tuple-element.39) | copy-start | bytes 49156
  89.7 1.6 %copy-start.13 = (f32[32,32,4]{1,2,0:T(4,128)S(1)}, f32[32,32,4]{1,2,0:T(4,128)}, u32[]{:S(2)}) copy-start(f32[32,32,4]{1,2,0:T(4,128)} %copy-done.12) | copy-start | bytes 49156
  89.7 2.4 %copy-start.15 = (f32[32,32,4]{1,2,0:T(4,128)S(1)}, f32[32,32,4]{1,2,0:T(4,128)}, u32[]{:S(2)}) copy-start(f32[32,32,4]{1,2,0:T(4,128)} %copy-done.14) | copy-start | bytes 49156
  91.2 1.8 %copy-start.11 = (f32[32,32,4]{1,0,2:T(8,128)S(1)}, f32[32,32,4]{1,0,2:T(8,128)}, u32[]{:S(2)}) copy-start(f32[32,32,4]{1,0,2:T(8,128)} %copy-done.10) | copy-start | bytes 49156
  91.2 2.1 %copy-start.9 = (f32[32,32,4]{1,0,2:T(8,128)S(1)}, f32[32,32,4]{1,0,2:T(8,128)}, u32[]{:S(2)}) copy-start(f32[32,32,4]{1,0,2:T(8,128)} %copy-done.8) | copy-start | bytes 49156
  107.5 1.8 %copy-start.7 = (f32[4,3,1024]{2,1,0:T(4,128)S(1)}, f32[4,3,1024]{2,1,0:T(4,128)}, u32[]{:S(2)}) copy-start(f32[4,3,1024]{2,1,0:T(4,128)} %copy-done.6) | copy-start | bytes 147460
  107.5 18.0 %copy-start.22 = (u32[32]{0:T(128)S(1)}, u32[32]{0:T(128)}, u32[]{:S(2)}) copy-start(u32[32]{0:T(128)} %constant.232) | copy-start | bytes 388
where the time goes:
time: 128 us
  blocking collectives  65.5 us (51%)
  other arithmetic  25.1 us (20%)
  matrix products  21.2 us (17%)
  local copies, waits for them, and re-layouts  14.8 us (12%)
    dot_general x2, matrix products, pair_kernel(): jnp.einsum('scp,tcp->pst', support, targets, precision=lax.Precision.HIGH...  20.9 us
    psum x1, blocking collectives, local(): predicted = lax.psum(product(theta.T, coeffs), 'sup')  16.9 us
    unnamed x1, blocking collectives  16.1 us
    all_gather x1, blocking collectives, local(): lax.all_gather(targets, 'sup', axis=0, tiled=True)  14.3 us
    all_gather x1, blocking collectives, local(): block = lax.all_gather(support, 'tgt', axis=0, tiled=True)  9.71 us
    all_gather x1, blocking collectives, local(): lax.all_gather(labels, 'sup', axis=0, tiled=True)  8.65 us
    div x6, other arithmetic, spread(): return summed / 9.0  6.42 us
    mul x2, other arithmetic, pair_kernel(): activated = 2.0 / math.pi * jnp.arcsin(correlation)  6 us

commit v1 on v0

--- a/solution.py
+++ b/solution.py
@@ -8,6 +8,16 @@
 DEPTH = 3
 WEIGHT_VAR = 1.6
 BIAS_VAR = 0.1
+
+
+def ring_gather(x, axis, dim):
+    ways, here, step = (lax.axis_size(axis), lax.axis_index(axis), x.shape[dim])
+    dims = [n * ways if d == dim else n for d, n in enumerate(x.shape)]
+    full = lax.dynamic_update_slice_in_dim(jnp.zeros(dims, x.dtype), x, here * step, axis=dim)
+    for far in range(1, ways):
+        x = lax.ppermute(x, axis, [(d, (d + 1) % ways) for d in range(ways)])
+        full = lax.dynamic_update_slice_in_dim(full, x, (here - far) % ways * step, axis=dim)
+    return full
 
 
 def spread(values):
@@ -73,7 +83,7 @@
     tgt_dev = targets.shape[0]
     block = lax.all_gather(support, "tgt", axis=0, tiled=True)
     group, group_labels = (
-        lax.all_gather(targets, "sup", axis=0, tiled=True),
+        ring_gather(targets, "sup", 0),
         lax.all_gather(labels, "sup", axis=0, tiled=True),
     )
     theta, pullback = jax.vjp(lambda images: pair_kernel(images, group), block)

time: 128 us -> 843 us (6.59)
  local copies, waits for them, and re-layouts: 14.8 us -> 654 us
  blocking collectives: 65.5 us -> 118 us
  waiting for transfers between devices: 0 us -> 21.7 us
    dynamic_update_slice x0 -> x8, local copies, waits for them, and re-layouts: none -> 621 us  [the longest x7 604 us: ring_gather(): lax.dynamic_update_slice_in_dim(full, x, (here - far) % ways * step, axis...]
    all_gather x1, blocking collectives: 8.65 us -> 79 us  [local(): lax.all_gather(labels, 'sup', axis=0, tiled=True)]
    ppermute x0 -> x7, waiting for transfers between devices: none -> 21.7 us  [ring_gather(): x = lax.ppermute(x, axis, [(d, (d + 1) % ways) for d in range(ways)])]
    all_gather x1 -> x0, blocking collectives: 14.3 us -> none  [local(): lax.all_gather(targets, 'sup', axis=0, tiled=True)]
    ppermute x0 -> x7, local copies, waits for them, and re-layouts: none -> 12.6 us  [ring_gather(): x = lax.ppermute(x, axis, [(d, (d + 1) % ways) for d in range(ways)])]
  transfers between devices with their start and end apart: 0 -> 7, of which waited for: 0 -> 5; matrix products, arithmetic and copies ran while one was open for 0% -> 66% of each run, Pallas kernels for 0% -> 0%
where the time goes in v1:
time: 843 us; the launch traced here: 839 us
  local copies, waits for them, and re-layouts  654 us (78%)
  blocking collectives  118 us (14%)
  other arithmetic  24.9 us (3%)
  waiting for transfers between devices  21.7 us (3%)
  matrix products  18 us (2%)
    dynamic_update_slice x7, local copies, waits for them, and re-layouts, ring_gather(): lax.dynamic_update_slice_in_dim(full, x, (here - far) % ways * step, axis...  604 us
    all_gather x1, blocking collectives, local(): lax.all_gather(labels, 'sup', axis=0, tiled=True)  79 us
    ppermute x7, waiting for transfers between devices, ring_gather(): x = lax.ppermute(x, axis, [(d, (d + 1) % ways) for d in range(ways)])  21.7 us
    dot_general x2, matrix products, pair_kernel(): jnp.einsum('scp,tcp->pst', support, targets, precision=lax.Precision.HIGH...  17.7 us
    dynamic_update_slice x1, local copies, waits for them, and re-layouts, ring_gather(): lax.dynamic_update_slice_in_dim(jnp.zeros(dims, x.dtype), x, here * step,...  17.5 us
  transfers between devices with their start and end apart: 7, of which 5 were waited for; matrix products, arithmetic and copies ran while one was open for 66% of the time, Pallas kernels for 0%

profile of v1, /device:TPU:0, one launch (start us, length us, event | category | flops | bytes accessed | tf_op | source)
XLA Modules:
  0.0 838.8 jit_solution(8868835632556208092)
XLA Ops:
  1.9 9.2 %all_gather.6 = f32[4,3,1024]{2,1,0:T(4,128)S(1)} all-gather(f32[1,3,1024]{2,1,0:T(4,128)S(1)} %copy.183), channel_id=1, replica_groups=mesh['tgt'=4,'sup'=8] {'tgt'}, dimensions={0}, use_global_device_ids=true | all-gather | bytes 61440 | tf_op jit(solution)/shard_map/all_gather | solution.py:84
  12.8 4.2 collective-permute-done.1
  17.2 4.7 collective-permute-done.2
  22.1 4.7 collective-permute-done.3
  27.7 4.0 collective-permute-done.4
  32.6 4.0 collective-permute-done.5
  43.7 17.5 %dynamic_update_slice.24 = f32[8,3,1024]{0,1,2:T(4,128)S(1)} dynamic-update-slice(f32[8,3,1024]{0,1,2:T(4,128)S(1)} %broadcast_in_dim.19, f32[1,3,1024]{0,1,2:T(4,128)} %copy.175, s32[]{:T(128)S(6)} %select_n.56, s32[]{:T(128)} %constant.136.clone.1, s32[]{:T(128)} %constant.136.clone.1) | dynamic-update-slice | bytes 24580 | tf_op jit(solution)/shard_map/dynamic_update_slice | solution.py:16
  61.2 79.0 %all-gather = f32[8,1,100]{2,1,0:T(1,128)S(1)} all-gather(f32[1,1,100]{2,1,0:T(1,128)S(1)} %bitcast.97), channel_id=1, replica_groups=mesh['tgt'=4,'sup'=8] {'sup'}, dimensions={0}, use_global_device_ids=true | all-gather | bytes 3600 | tf_op jit(solution)/shard_map/all_gather | solution.py:87
  140.2 2.2 copy.176
  142.4 86.3 %dynamic_update_slice.25 = f32[8,3,1024]{0,1,2:T(4,128)S(1)} dynamic-update-slice(f32[8,3,1024]{0,1,2:T(4,128)S(1)} %dynamic_update_slice.24, f32[1,3,1024]{0,1,2:T(4,128)} %copy.176, s32[]{:T(128)S(6)} %select_n.58, s32[]{:T(128)} %constant.136.clone.1, s32[]{:T(128)} %constant.136.clone.1) | dynamic-update-slice | bytes 24580 | tf_op jit(solution)/shard_map/dynamic_update_slice | solution.py:19
  228.7 1.7 copy.177
  230.4 86.3 %dynamic_update_slice.26 = f32[8,3,1024]{0,1,2:T(4,128)S(1)} dynamic-update-slice(f32[8,3,1024]{0,1,2:T(4,128)S(1)} %dynamic_update_slice.25, f32[1,3,1024]{0,1,2:T(4,128)} %copy.177, s32[]{:T(128)S(6)} %select_n.60, s32[]{:T(128)} %constant.136.clone.1, s32[]{:T(128)} %constant.136.clone.1) | dynamic-update-slice | bytes 24580 | tf_op jit(solution)/shard_map/dynamic_update_slice | solution.py:19
  316.7 1.7 copy.178
  318.4 86.3 %dynamic_update_slice.27 = f32[8,3,1024]{0,1,2:T(4,128)S(1)} dynamic-update-slice(f32[8,3,1024]{0,1,2:T(4,128)S(1)} %dynamic_update_slice.26, f32[1,3,1024]{0,1,2:T(4,128)} %copy.178, s32[]{:T(128)S(6)} %select_n.62, s32[]{:T(128)} %constant.136.clone.1, s32[]{:T(128)} %constant.136.clone.1) | dynamic-update-slice | bytes 24580 | tf_op jit(solution)/shard_map/dynamic_update_slice | solution.py:19
  404.7 1.7 copy.179
  406.4 86.3 %dynamic_update_slice.28 = f32[8,3,1024]{0,1,2:T(4,128)S(1)} dynamic-update-slice(f32[8,3,1024]{0,1,2:T(4,128)S(1)} %dynamic_update_slice.27, f32[1,3,1024]{0,1,2:T(4,128)} %copy.179, s32[]{:T(128)S(6)} %select_n.64, s32[]{:T(128)} %constant.136.clone.1, s32[]{:T(128)} %constant.136.clone.1) | dynamic-update-slice | bytes 24580 | tf_op jit(solution)/shard_map/dynamic_update_slice | solution.py:19
  492.7 1.7 copy.180
  494.4 86.3 %dynamic_update_slice.29 = f32[8,3,1024]{0,1,2:T(4,128)S(1)} dynamic-update-slice(f32[8,3,1024]{0,1,2:T(4,128)S(1)} %dynamic_update_slice.28, f32[1,3,1024]{0,1,2:T(4,128)} %copy.180, s32[]{:T(128)S(6)} %select_n.66, s32[]{:T(128)} %constant.136.clone.1, s32[]{:T(128)} %constant.136.clone.1) | dynamic-update-slice | bytes 24580 | tf_op jit(solution)/shard_map/dynamic_update_slice | solution.py:19
  580.7 1.7 copy.181
  582.4 86.3 %dynamic_update_slice.30 = f32[8,3,1024]{0,1,2:T(4,128)S(1)} dynamic-update-slice(f32[8,3,1024]{0,1,2:T(4,128)S(1)} %dynamic_update_slice.29, f32[1,3,1024]{0,1,2:T(4,128)} %copy.181, s32[]{:T(128)S(6)} %select_n.68, s32[]{:T(128)} %constant.136.clone.1, s32[]{:T(128)} %constant.136.clone.1) | dynamic-update-slice | bytes 24580 | tf_op jit(solution)/shard_map/dynamic_update_slice | solution.py:19
  668.7 1.7 copy.182
  670.4 86.3 %dynamic_update_slice.31 = f32[8,3,1024]{0,1,2:T(4,128)S(1)} dynamic-update-slice(f32[8,3,1024]{0,1,2:T(4,128)S(1)} %dynamic_update_slice.30, f32[1,3,1024]{0,1,2:T(4,128)} %copy.182, s32[]{:T(128)S(6)} %select_n.70, s32[]{:T(128)} %constant.136.clone.1, s32[]{:T(128)} %constant.136.clone.1) | dynamic-update-slice | bytes 24580 | tf_op jit(solution)/shard_map/dynamic_update_slice | solution.py:19
  758.3 8.4 multiply_bitcast_fusion
  766.6 1.8 copy.185
  772.1 3.3 add_multiply_fusion.3
  775.4 3.3 add_multiply_fusion.1
  778.7 2.8 multiply_reduce_fusion.1
  781.9 13.8 %psum.7 = f32[8,100]{1,0:T(8,128)S(1)} all-reduce(f32[8,100]{1,0:T(8,128)S(1)} %fusion.154), channel_id=1, replica_groups=mesh['tgt'=4,'sup'=8] {'sup'}, use_global_device_ids=true, to_apply=%region_3.4 | all-reduce | flops 800 | bytes 6400 | tf_op jit(solution)/shard_map/psum | solution.py:90
  808.0 2.0 copy.212
  810.0 9.3 %fusion.155 = f32[1024,4,3]{1,2,0:T(4,128)} fusion(f32[1024,4,8]{2,1,0:T(4,128)} %copy.212, f32[8,3,1024]{0,1,2:T(4,128)S(1)} %dynamic_update_slice.31), kind=kOutput, calls=%fused_computation.322 | convolution fusion | flops 1179648 | bytes 278528 | tf_op jit(solution)/shard_map/transpose(jvp(scp,tcp->pst))/dot_general | solution.py:54
  819.3 1.8 copy.213
  821.2 16.0 %all-reduce.63 = f32[4,3,1024]{2,1,0:T(4,128)S(1)} all-reduce(f32[4,3,1024]{2,1,0:T(4,128)S(1)} %copy.223), channel_id=2, replica_groups=mesh['tgt'=4,'sup'=8] {'tgt'}, use_global_device_ids=true, to_apply=%region_7.8.clone | all-reduce | flops 12288 | bytes 98304
  (137 shorter events, 30.9 us)
Async XLA Ops:
  0.6 781.1 %copy-start = (f32[4,100]{1,0:T(4,128)S(1)}, f32[4,100]{1,0:T(4,128)}, u32[]{:S(2)}) copy-start(f32[4,100]{1,0:T(4,128)} %param.5) | copy-start | bytes 4804
  0.6 11.4 %collective-permute-start = (f32[1,3,1024]{2,0,1:T(1,128)}, f32[1,3,1024]{2,0,1:T(1,128)S(1)}, u32[]{:S(2)}, u32[]{:S(2)}) collective-permute-start(f32[1,3,1024]{2,0,1:T(1,128)} %param.6), channel_id=1, source_target_pairs={{0,1},{1,2},{2,3},{3,4},{4,5},{5,6},{6,7},{7,0},{8,9},{9,10},{10,1... | collective-permute-start | bytes 36872 | tf_op jit(solution)/shard_map/ppermute | solution.py:18
  11.1 28.0 %copy-start.16 = (f32[4,3,1024]{2,1,0:T(4,128)}, f32[4,3,1024]{2,1,0:T(4,128)S(1)}, u32[]{:S(2)}) copy-start(f32[4,3,1024]{2,1,0:T(4,128)S(1)} %all_gather.6) | copy-start | bytes 147460
  11.4 26.0 %copy-start.27 = (f32[1,3,1024]{2,0,1:T(1,128)S(1)}, f32[1,3,1024]{2,0,1:T(1,128)}, u32[]{:S(2)}) copy-start(f32[1,3,1024]{2,0,1:T(1,128)} %param.6) | copy-start | bytes 36868
  12.0 5.0 collective-permute-start.1
  17.0 4.9 collective-permute-start.2
  17.2 4.7 copy-start.20
  21.9 4.9 collective-permute-start.3
  26.8 4.9 collective-permute-start.4
  31.7 4.9 collective-permute-start.5
  36.7 632.0 %collective-permute-start.6 = (f32[1,3,1024]{2,0,1:T(1,128)S(1)}, f32[1,3,1024]{2,0,1:T(1,128)S(1)}, u32[]{:S(2)}, u32[]{:S(2)}) collective-permute-start(f32[1,3,1024]{2,0,1:T(1,128)S(1)} %collective-permute-done.5), channel_id=1, source_target_pairs={{0,1},{1,2},{2,3},{3,4},{4,5},{5,6},{6,7},{7,0},{8,9},{9,10},{10,1... | collective-permute-start | bytes 36872 | tf_op jit(solution)/shard_map/ppermute | solution.py:18
  37.5 5.4 copy-start.29
  43.7 17.5 %copy-start.28 = (f32[1,100]{1,0:T(1,128)S(1)}, f32[1,100]{1,0:T(1,128)}, u32[]{:S(2)}) copy-start(f32[1,100]{1,0:T(1,128)} %param.7) | copy-start | bytes 1204
  756.7 1.6 copy-start.1
  769.5 2.0 copy-start.24
  769.5 2.1 copy-start.22
  770.1 1.6 copy-start.26
  771.6 3.9 copy-start.3
  771.6 3.8 copy-start.5
  771.7 7.0 copy-start.9
  771.7 7.0 copy-start.11
  796.4 2.7 copy-start.2
  799.0 1.5 copy-start.14
  800.5 1.9 copy-start.4
  800.5 1.9 copy-start.6
  800.5 1.9 copy-start.8
  800.5 1.9 copy-start.15
  802.4 1.5 copy-start.25
  802.5 2.3 copy-start.23
  803.9 1.8 copy-start.21
  803.9 2.1 copy-start.19
  819.3 1.8 copy-start.17
  (5 other events, 6.1 us)
